TPU v7x, 32 devices: a whole 2x2x4 slice. The times are simulated.
32 devices in a mesh: expert: 8 (over y, x, core), tensor: 4 (over z).
Axes of the slice: x: 2, y: 2, z: 4, core: 2. Of those that a mesh axis runs over, the one named last changes fastest.
Arguments:
- tokens: bfloat16 [2560, 4096], P('expert', 'tensor'), may hold values from -6 to 6
- grad_out: bfloat16 [2560, 4096], P('expert', 'tensor'), may hold values from -6 to 6
- routes: int32 [2560, 4], P('expert'), may hold values from 0 to 7, all different within a row; in each aligned block of 320 rows (0 to 319, 320 to 639, ...) at most 200 rows name the same one
- route_weights: float32 [2560, 4], P('expert'), may hold values from 0.05 to 0.5
- swap_flags: int32 [4], replicated, may hold values from 0 to 1023
- weights: bfloat16 [8, 3, 1536, 4096], P('expert', None, None, 'tensor'), may hold values from -0.09375 to 0.09375
- first_moment: bfloat16 [8, 3, 1536, 4096], P('expert', None, None, 'tensor'), may hold values from -8 to 8
- second_moment: bfloat16 [8, 3, 1536, 4096], P('expert', None, None, 'tensor'), may hold values from 1 to 30
Outputs:
- combined: bfloat16 [2560, 4096], P('expert', 'tensor')
- update: bfloat16 [8, 3, 1536, 4096], P('expert', None, None, 'tensor')
Inputs may be any that keep to these rules, and one draw needn't show every extreme that they name: `routes`: in each aligned block of 320 rows no expert is named by more than 200 rows, a bound that some block reaches; a row names 4 different experts.
All inputs are finite; a program needn't handle non-finite values.
Results may differ from a plain program's by a relative error of at most 0.023.
Values may be sent and summed in bfloat16 or wider, within the bound.
A program may use at most 192 MiB of HBM per device.

v0:
```python
import functools
import jax
import jax.numpy as jnp
from jax import lax
from jax.experimental import pallas as pl
from jax.experimental.pallas import tpu as pltpu
from jax.sharding import PartitionSpec as P

MESH = pl.DeviceIdType.MESH
COLS = 128
SUB = 4
LAG = 2
ONE = 1.0 / (1.0 - 0.9**20)
TWO = 1.0 / (1.0 - 0.95**20)


def contract_last(left_rows, right_rows):
    return lax.dot_general(
        left_rows, right_rows, (((1,), (1,)), ((), ())), preferred_element_type=jnp.float32
    )


def contract_first(left_rows, right_rows):
    return lax.dot_general(
        left_rows, right_rows, (((0,), (0,)), ((), ())), preferred_element_type=jnp.float32
    )


def flip(spot, other, count):
    total, bit = 0, 1
    while bit < count:
        total = total + bit * lax.rem(lax.div(spot, bit) + lax.div(other, bit), 2)
        bit *= 2
    return total


def kernel(
    groups, line, ring, passes,
    tokens, grads, routes, route_w, trade, weights, first, second,
    combined, update,
    counted, ranks, shares, masks, xs, gs, send_x, send_g, returned, out_sum, wv, total,
    own, came, moment, square, mine, theirs, comb,
    x_send, x_recv, g_send, g_recv, o_send, o_recv,
    in_send, in_recv, out_send, w_sem, m_sem, u_send, u_recv, u_out,
):
    toks, width = tokens.shape
    rows = xs.shape[1]
    units = passes * groups * SUB
    blocks = passes * SUB
    half = line // 2
    inner = half - 1
    me = lax.axis_index("expert")
    spot = lax.axis_index("tensor")
    near = (spot < half).astype(jnp.int32)
    depth = near * spot + (1 - near) * (line - 1 - spot)
    inward = spot + 2 * near - 1
    outward = spot + 1 - 2 * near
    is_mid = (depth == inner).astype(jnp.int32)
    lag_total = LAG * (half + inner - depth)
    partner = flip(me, jnp.int32(1), groups)

    def w_copy(m):
        return pltpu.make_async_copy(
            weights.at[0, :, pl.ds(m * COLS, COLS), :], wv.at[m], w_sem.at[m]
        )

    def m_copies(m):
        k = lax.rem(m, 2)
        cut = pl.ds(pl.multiple_of(m * COLS, COLS), COLS)
        return (
            pltpu.make_async_copy(first.at[0, :, cut, :], moment.at[k], m_sem.at[0, k]),
            pltpu.make_async_copy(second.at[0, :, cut, :], square.at[k], m_sem.at[1, k]),
        )

    def x_copy(j):
        return pltpu.make_async_remote_copy(
            send_x.at[j], xs.at[j], x_send.at[j], x_recv.at[j],
            device_id={"expert": flip(me, j, groups)}, device_id_type=MESH,
        )

    def g_copy(j):
        return pltpu.make_async_remote_copy(
            send_g.at[j], gs.at[j], g_send.at[j], g_recv.at[j],
            device_id={"expert": flip(me, j, groups)}, device_id_type=MESH,
        )

    def o_copy(j):
        return pltpu.make_async_remote_copy(
            send_x.at[j], returned.at[j], o_send.at[j], o_recv.at[j],
            device_id={"expert": flip(me, j, groups)}, device_id_type=MESH,
        )

    def in_copy(slot):
        return pltpu.make_async_remote_copy(
            own.at[slot], came.at[is_mid, slot], in_send.at[slot], in_recv.at[is_mid, slot],
            device_id={"tensor": inward}, device_id_type=MESH,
        )

    def out_copy(slot):
        return pltpu.make_async_remote_copy(
            came.at[1, slot], came.at[1, slot], out_send.at[slot], in_recv.at[1, slot],
            device_id={"tensor": outward}, device_id_type=MESH,
        )

    def arrived(kind, slot):
        pltpu.make_async_remote_copy(
            own.at[slot], came.at[kind, slot], in_send.at[slot], in_recv.at[kind, slot],
            device_id={"tensor": inward}, device_id_type=MESH,
        ).wait_recv()

    def u_copy(k):
        return pltpu.make_async_remote_copy(
            mine.at[k], theirs.at[k], u_send.at[k], u_recv.at[k],
            device_id={"expert": partner}, device_id_type=MESH,
        )

    def u_store(m):
        k = lax.rem(m, 2)
        cut = pl.ds(pl.multiple_of(m * COLS, COLS), COLS)
        return pltpu.make_async_copy(mine.at[k], update.at[0, :, cut, :], u_out.at[k])

    for m in range(blocks):
        w_copy(m).start()
    for m in range(2):
        for copy in m_copies(m):
            copy.start()

    lane = lax.broadcasted_iota(jnp.int32, (toks, 128), 1)
    hits = jnp.zeros((toks, 128), jnp.float32)
    share = jnp.zeros((toks, 128), jnp.float32)
    for r in range(routes.shape[1]):
        hit = routes[:, r : r + 1] == lane
        hits = hits + jnp.where(hit, 1.0, 0.0)
        share = share + jnp.where(hit, route_w[:, r : r + 1], 0.0)
    counted[...] = hits
    shares[...] = share
    later = lax.broadcasted_iota(jnp.int32, (toks, toks), 0)
    sooner = lax.broadcasted_iota(jnp.int32, (toks, toks), 1)
    below = jnp.where(sooner < later, 1.0, 0.0).astype(jnp.bfloat16)
    ranks[...] = jnp.dot(below, hits.astype(jnp.bfloat16), preferred_element_type=jnp.float32)

    def column(table, expert):
        return jnp.sum(jnp.where(lane == expert, table[...], 0.0), axis=1, keepdims=True)

    def dispatch(j):
        expert = flip(me, j, groups)
        place = jnp.where(column(counted, expert) > 0.5, column(ranks, expert), -1.0)
        slot = lax.broadcasted_iota(jnp.int32, (toks, rows), 1)
        mask = jnp.where(place.astype(jnp.int32) == slot, 1.0, 0.0).astype(jnp.bfloat16)
        masks[j] = mask
        scaled = (column(shares, expert) * grads[...].astype(jnp.float32)).astype(jnp.bfloat16)
        picked = contract_first(mask, tokens[...]).astype(jnp.bfloat16)
        scaled_picked = contract_first(mask, scaled).astype(jnp.bfloat16)

        @pl.when(j == 0)
        def _():
            xs[0] = picked
            gs[0] = scaled_picked

        @pl.when(j > 0)
        def _():
            send_x[j] = picked
            send_g[j] = scaled_picked
            x_copy(j).start()
            g_copy(j).start()

    def split(u):
        span = groups * SUB
        big = lax.div(u, span)
        rest = lax.rem(u, span)
        place = lax.div(rest, SUB)
        turn = (big == passes - 1).astype(jnp.int32)
        return big, place, place + turn * (groups - 1 - 2 * place), lax.rem(rest, SUB)

    def settle(m):
        k = lax.rem(m, 2)
        u_copy(k).wait()
        swap = trade[...] > 0

        def piece(s, _):
            cut = pl.ds(pl.multiple_of(s * 16, 16), 16)
            for q in range(3):
                kept = mine[k, q, cut, :].astype(jnp.float32)
                moved = theirs[k, q, cut, :].astype(jnp.float32)
                mine[k, q, cut, :] = jnp.where(swap, moved, kept).astype(jnp.bfloat16)
            return 0

        lax.fori_loop(0, COLS // 16, piece, 0)
        u_store(m).start()

    def adam(m, b):
        k = lax.rem(m, 2)

        @pl.when(m > 0)
        def _():
            settle(m - 1)

        @pl.when(m > 1)
        def _():
            u_store(m - 2).wait()

        for copy in m_copies(m):
            copy.wait()

        def piece(s, _):
            cut = pl.ds(pl.multiple_of(s * 16, 16), 16)
            for q in range(3):
                grad = total[b, q, cut, :]
                moment_new = 0.9 * moment[k, q, cut, :].astype(jnp.float32) + 0.1 * grad
                square_new = 0.95 * square[k, q, cut, :].astype(jnp.float32) + 0.05 * grad * grad
                step = moment_new * ONE / (jnp.sqrt(square_new * TWO) + 1e-08)
                mine[k, q, cut, :] = step.astype(jnp.bfloat16)
            return 0

        lax.fori_loop(0, COLS // 16, piece, 0)
        u_copy(k).start()

        @pl.when(m + 2 < blocks)
        def _():
            for copy in m_copies(m + 2):
                copy.start()

    def start_unit(u):
        big, place, j, b = split(u)
        slot = lax.rem(u, ring)
        m = big * SUB + b

        @pl.when((big == 0) & (b == 0) & (j > 0))
        def _():
            x_copy(j).wait_recv()
            g_copy(j).wait_recv()

        @pl.when(place == 0)
        def _():
            w_copy(m).wait()

        @pl.when(u >= ring)
        def _():
            in_copy(slot).wait_send()

        both = contract_last(xs[j], wv[m, 0:2].reshape(2 * COLS, width))
        own[slot, :, 0 : 2 * COLS] = both.astype(jnp.bfloat16)
        own[slot, :, 2 * COLS :] = contract_last(gs[j], wv[m, 2]).astype(jnp.bfloat16)

        @pl.when(depth == 0)
        def _():
            in_copy(slot).start()

    def pass_unit(u):
        slot = lax.rem(u, ring)
        arrived(0, slot)
        own[slot] = (
            own[slot].astype(jnp.float32) + came[0, slot].astype(jnp.float32)
        ).astype(jnp.bfloat16)
        in_copy(slot).start()

    def finish_unit(u):
        big, place, j, b = split(u)
        slot = lax.rem(u, ring)
        m = big * SUB + b
        arrived(1, slot)

        @pl.when(depth == inner)
        def _():
            came[1, slot] = (
                own[slot].astype(jnp.float32) + came[1, slot].astype(jnp.float32)
            ).astype(jnp.bfloat16)

        @pl.when(depth > 0)
        def _():
            @pl.when(u >= 2)
            def _():
                out_copy(lax.rem(u - 2, ring)).wait_send()

            out_copy(slot).start()

        gate = came[1, slot, :, 0:COLS].astype(jnp.float32)
        up = came[1, slot, :, COLS : 2 * COLS].astype(jnp.float32)
        back = came[1, slot, :, 2 * COLS :].astype(jnp.float32)
        sig = jax.nn.sigmoid(gate)
        hidden = (gate * sig * up).astype(jnp.bfloat16)
        gate_grad = (back * up * sig * (1.0 + gate * (1.0 - sig))).astype(jnp.bfloat16)
        up_grad = (back * gate * sig).astype(jnp.bfloat16)
        out = jnp.dot(hidden, wv[m, 2], preferred_element_type=jnp.float32)

        @pl.when(m == 0)
        def _():
            out_sum[j] = out

        @pl.when(m > 0)
        def _():
            out_sum[j] += out

        pair = jnp.concatenate([gate_grad, up_grad], axis=1)
        pair_sum = contract_first(pair, xs[j]).reshape(2, COLS, width)
        down_sum = contract_first(hidden, gs[j])

        @pl.when(place == 0)
        def _():
            total[b, 0:2] = pair_sum
            total[b, 2] = down_sum

        @pl.when(place > 0)
        def _():
            total[b, 0:2] += pair_sum
            total[b, 2] += down_sum

        @pl.when(m == blocks - 1)
        def _():
            @pl.when(j > 0)
            def _():
                x_copy(j).wait_send()
                send_x[j] = out_sum[j].astype(jnp.bfloat16)
                o_copy(j).start()

            @pl.when(j == 0)
            def _():
                returned[0] = out_sum[0].astype(jnp.bfloat16)

        @pl.when(place == groups - 1)
        def _():
            adam(m, b)

    def step(i, _):
        @pl.when(i < groups)
        def _():
            dispatch(i)

        @pl.when(i < units)
        def _():
            start_unit(i)

        @pl.when((depth > 0) & (i >= LAG * depth) & (i - LAG * depth < units))
        def _():
            pass_unit(i - LAG * depth)

        @pl.when((i >= lag_total) & (i - lag_total < units))
        def _():
            finish_unit(i - lag_total)

        return 0

    lax.fori_loop(0, units + LAG * (line - 1), step, 0)

    comb[...] = jnp.zeros_like(comb)

    def gather(place, _):
        j = groups - 1 - place

        @pl.when(j > 0)
        def _():
            o_copy(j).wait()
            g_copy(j).wait_send()

        expert = flip(me, j, groups)
        rows_back = jnp.dot(masks[j], returned[j], preferred_element_type=jnp.float32)
        comb[...] += column(shares, expert) * rows_back
        return 0

    lax.fori_loop(0, groups, gather, 0)
    combined[...] = comb[...].astype(jnp.bfloat16)

    settle(blocks - 1)
    for m in (blocks - 2, blocks - 1):
        u_store(m).wait()
    for back in range(min(ring, units)):
        in_copy((units - 1 - back) % ring).wait_send()

    @pl.when(depth > 0)
    def _():
        for u in (units - 2, units - 1):
            out_copy(u % ring).wait_send()


def body(tokens, grad_out, routes, route_weights, swap_flags, weights, first_moment, second_moment):
    groups, line = lax.axis_size("expert"), lax.axis_size("tensor")
    toks, width = tokens.shape
    hidden_width = weights.shape[2]
    cap = toks * routes.shape[1] * 5 // (4 * groups)
    rows = -(-cap // 16) * 16
    passes = hidden_width // (COLS * SUB)
    blocks = passes * SUB
    ring = LAG * (line - 1) + 3
    me = lax.axis_index("expert")
    paired = jnp.repeat(jnp.bitwise_and(swap_flags, 1), 2)
    traded = jnp.sum(jnp.where(jnp.arange(groups) == me, paired, 0))
    trade = jnp.broadcast_to(traded.astype(jnp.int32), (16, width))
    bf, f32 = jnp.bfloat16, jnp.float32
    dma = pltpu.SemaphoreType.DMA
    whole = pl.BlockSpec(memory_space=pltpu.VMEM)
    left = pl.BlockSpec(memory_space=pl.ANY)
    flops = 2 * groups * rows * width * hidden_width * 7
    combined, update = pl.pallas_call(
        functools.partial(kernel, groups, line, ring, passes),
        out_shape=(
            jax.ShapeDtypeStruct((toks, width), bf),
            jax.ShapeDtypeStruct(weights.shape, bf),
        ),
        in_specs=[whole] * 5 + [left] * 3,
        out_specs=(whole, left),
        scratch_shapes=[
            pltpu.VMEM((toks, 128), f32),
            pltpu.VMEM((toks, 128), f32),
            pltpu.VMEM((toks, 128), f32),
            pltpu.VMEM((groups, toks, rows), bf),
            pltpu.VMEM((groups, rows, width), bf),
            pltpu.VMEM((groups, rows, width), bf),
            pltpu.VMEM((groups, rows, width), bf),
            pltpu.VMEM((groups, rows, width), bf),
            pltpu.VMEM((groups, rows, width), bf),
            pltpu.VMEM((groups, rows, width), f32),
            pltpu.VMEM((blocks, 3, COLS, width), bf),
            pltpu.VMEM((SUB, 3, COLS, width), f32),
            pltpu.VMEM((ring, rows, 3 * COLS), bf),
            pltpu.VMEM((2, ring, rows, 3 * COLS), bf),
            pltpu.VMEM((2, 3, COLS, width), bf),
            pltpu.VMEM((2, 3, COLS, width), bf),
            pltpu.VMEM((2, 3, COLS, width), bf),
            pltpu.VMEM((2, 3, COLS, width), bf),
            pltpu.VMEM((toks, width), f32),
            dma((groups,)), dma((groups,)), dma((groups,)), dma((groups,)),
            dma((groups,)), dma((groups,)),
            dma((ring,)), dma((2, ring)), dma((ring,)),
            dma((blocks,)), dma((2, 2)), dma((2,)), dma((2,)), dma((2,)),
        ],
        compiler_params=pltpu.CompilerParams(
            has_side_effects=True, vmem_limit_bytes=66_000_000
        ),
        cost_estimate=pl.CostEstimate(
            flops=flops, bytes_accessed=8 * weights.size, transcendentals=0
        ),
    )(tokens, grad_out, routes, route_weights, trade, weights, first_moment, second_moment)
    return combined, update


def solution(mesh):
    placed = (
        P("expert", "tensor"),
        P("expert", "tensor"),
        P("expert", None),
        P("expert", None),
        P(),
        P("expert", None, None, "tensor"),
        P("expert", None, None, "tensor"),
        P("expert", None, None, "tensor"),
    )
    return jax.shard_map(
        body,
        mesh=mesh,
        in_specs=placed,
        out_specs=(P("expert", "tensor"), P("expert", None, None, "tensor")),
        check_vma=False,
    )
```

profile of v0, /device:TPU:0, one launch (start us, length us, event | category | flops | bytes accessed | tf_op | source)
XLA Modules:
  0.0 396.6 jit_solution(4341048422188302277)
XLA Ops:
  0.6 0.7 broadcast_and_fusion
  1.3 0.6 fusion
  1.9 1.3 broadcast_in_dim.12.trade
  3.2 1.5 copy.12.routes
  4.7 1.5 copy.13.route_w
  6.2 379.9 %shard_map.95 = (bf16[320,1024]{1,0:T(8,128)(2,1)}, bf16[1,3,1536,1024]{3,2,1,0:T(8,128)(2,1)}) custom-call(bf16[320,1024]{1,0:T(8,128)(2,1)} %tokens.1, bf16[320,1024]{1,0:T(8,128)(2,1)} %grads.1, s32[320,4]{1,0:T(8,128)} %copy.12.routes, f32[320,4]{1,0:T(8,128)} %copy.13.route_w, s32[16,1024]{1,0:T(8,128)} %broadcast_in_dim.12.trade, ...), custom_call_target="tpu_custom_call" | custom-call | flops 36641439744 | bytes 37748736 | tf_op jit(solution)/shard_map/pallas_call | solution.py:393
  386.1 2.0 copy.16
  388.1 8.5 %copy.17 = bf16[1,3,1536,1024]{3,2,1,0:T(8,128)(2,1)} copy(bf16[1,3,1536,1024]{3,2,1,0:T(8,128)(2,1)} %get-tuple-element.5) | data formatting | bytes 18874368
where the time goes:
time: 397 us
  Pallas kernels  380 us (96%)
  local copies, waits for them, and re-layouts  14.8 us (4%)
    pallas_call x1, Pallas kernels, body(): pl.pallas_call(functools.partial(kernel, groups, line, ring, passes), out...  380 us
    unnamed x4, local copies, waits for them, and re-layouts  13.5 us

commit v1 on v0

--- a/solution.py
+++ b/solution.py
@@ -8,7 +8,7 @@
 
 MESH = pl.DeviceIdType.MESH
 COLS = 128
-SUB = 4
+SUB = 6
 LAG = 2
 ONE = 1.0 / (1.0 - 0.9**20)
 TWO = 1.0 / (1.0 - 0.95**20)
@@ -35,11 +35,11 @@
 
 
 def kernel(
-    groups, line, ring, passes,
-    tokens, grads, routes, route_w, trade, weights, first, second,
-    combined, update,
+    groups, line, ring, passes, cap,
+    tokens, grads, routes, route_w, weights, first, second,
+    combined, both_steps,
     counted, ranks, shares, masks, xs, gs, send_x, send_g, returned, out_sum, wv, total,
-    own, came, moment, square, mine, theirs, comb,
+    own, came, moment, square, mine, comb,
     x_send, x_recv, g_send, g_recv, o_send, o_recv,
     in_send, in_recv, out_send, w_sem, m_sem, u_send, u_recv, u_out,
 ):
@@ -57,6 +57,7 @@
     outward = spot + 1 - 2 * near
     is_mid = (depth == inner).astype(jnp.int32)
     lag_total = LAG * (half + inner - depth)
+    filled = pl.ds(0, -(-cap // 8) * 8)
     partner = flip(me, jnp.int32(1), groups)
 
     def w_copy(m):
@@ -92,55 +93,61 @@
 
     def in_copy(slot):
         return pltpu.make_async_remote_copy(
-            own.at[slot], came.at[is_mid, slot], in_send.at[slot], in_recv.at[is_mid, slot],
+            own.at[slot, filled], came.at[is_mid, slot, filled], in_send.at[slot], in_recv.at[is_mid, slot],
             device_id={"tensor": inward}, device_id_type=MESH,
         )
 
     def out_copy(slot):
         return pltpu.make_async_remote_copy(
-            came.at[1, slot], came.at[1, slot], out_send.at[slot], in_recv.at[1, slot],
+            came.at[1, slot, filled], came.at[1, slot, filled], out_send.at[slot], in_recv.at[1, slot],
             device_id={"tensor": outward}, device_id_type=MESH,
         )
 
     def arrived(kind, slot):
         pltpu.make_async_remote_copy(
-            own.at[slot], came.at[kind, slot], in_send.at[slot], in_recv.at[kind, slot],
+            own.at[slot, filled], came.at[kind, slot, filled], in_send.at[slot], in_recv.at[kind, slot],
             device_id={"tensor": inward}, device_id_type=MESH,
         ).wait_recv()
 
-    def u_copy(k):
-        return pltpu.make_async_remote_copy(
-            mine.at[k], theirs.at[k], u_send.at[k], u_recv.at[k],
-            device_id={"expert": partner}, device_id_type=MESH,
-        )
-
-    def u_store(m):
+    def u_copies(m):
         k = lax.rem(m, 2)
         cut = pl.ds(pl.multiple_of(m * COLS, COLS), COLS)
-        return pltpu.make_async_copy(mine.at[k], update.at[0, :, cut, :], u_out.at[k])
-
+        return (
+            pltpu.make_async_copy(mine.at[k], both_steps.at[0, :, cut, :], u_out.at[k]),
+            pltpu.make_async_remote_copy(
+                mine.at[k], both_steps.at[1, :, cut, :], u_send.at[k], u_recv.at[m],
+                device_id={"expert": partner}, device_id_type=MESH,
+            ),
+        )
+
+    comb[...] = jnp.zeros_like(comb)
     for m in range(blocks):
         w_copy(m).start()
     for m in range(2):
         for copy in m_copies(m):
             copy.start()
 
-    lane = lax.broadcasted_iota(jnp.int32, (toks, 128), 1)
-    hits = jnp.zeros((toks, 128), jnp.float32)
-    share = jnp.zeros((toks, 128), jnp.float32)
-    for r in range(routes.shape[1]):
-        hit = routes[:, r : r + 1] == lane
+    lane = lax.broadcasted_iota(jnp.int32, (128, toks), 0)
+    hits = jnp.zeros((128, toks), jnp.float32)
+    share = jnp.zeros((128, toks), jnp.float32)
+    for r in range(routes.shape[0]):
+        hit = routes[r : r + 1, :] == lane
         hits = hits + jnp.where(hit, 1.0, 0.0)
-        share = share + jnp.where(hit, route_w[:, r : r + 1], 0.0)
-    counted[...] = hits
-    shares[...] = share
+        share = share + jnp.where(hit, route_w[r : r + 1, :], 0.0)
     later = lax.broadcasted_iota(jnp.int32, (toks, toks), 0)
     sooner = lax.broadcasted_iota(jnp.int32, (toks, toks), 1)
-    below = jnp.where(sooner < later, 1.0, 0.0).astype(jnp.bfloat16)
-    ranks[...] = jnp.dot(below, hits.astype(jnp.bfloat16), preferred_element_type=jnp.float32)
+    same = jnp.where(sooner == later, 1.0, 0.0)
+    below = jnp.where(sooner < later, 1.0, 0.0)
+    counted[...] = contract_last(same.astype(jnp.bfloat16), hits.astype(jnp.bfloat16))
+    ranks[...] = contract_last(below.astype(jnp.bfloat16), hits.astype(jnp.bfloat16))
+    shares[...] = lax.dot_general(
+        same, share, (((1,), (1,)), ((), ())),
+        precision=lax.Precision.HIGHEST, preferred_element_type=jnp.float32,
+    )
 
     def column(table, expert):
-        return jnp.sum(jnp.where(lane == expert, table[...], 0.0), axis=1, keepdims=True)
+        across = lax.broadcasted_iota(jnp.int32, (toks, 128), 1)
+        return jnp.sum(jnp.where(across == expert, table[...], 0.0), axis=1, keepdims=True)
 
     def dispatch(j):
         expert = flip(me, j, groups)
@@ -172,32 +179,14 @@
         turn = (big == passes - 1).astype(jnp.int32)
         return big, place, place + turn * (groups - 1 - 2 * place), lax.rem(rest, SUB)
 
-    def settle(m):
-        k = lax.rem(m, 2)
-        u_copy(k).wait()
-        swap = trade[...] > 0
-
-        def piece(s, _):
-            cut = pl.ds(pl.multiple_of(s * 16, 16), 16)
-            for q in range(3):
-                kept = mine[k, q, cut, :].astype(jnp.float32)
-                moved = theirs[k, q, cut, :].astype(jnp.float32)
-                mine[k, q, cut, :] = jnp.where(swap, moved, kept).astype(jnp.bfloat16)
-            return 0
-
-        lax.fori_loop(0, COLS // 16, piece, 0)
-        u_store(m).start()
-
     def adam(m, b):
         k = lax.rem(m, 2)
 
-        @pl.when(m > 0)
-        def _():
-            settle(m - 1)
-
         @pl.when(m > 1)
         def _():
-            u_store(m - 2).wait()
+            keep, give = u_copies(m - 2)
+            keep.wait()
+            give.wait_send()
 
         for copy in m_copies(m):
             copy.wait()
@@ -213,12 +202,25 @@
             return 0
 
         lax.fori_loop(0, COLS // 16, piece, 0)
-        u_copy(k).start()
+        for copy in u_copies(m):
+            copy.start()
 
         @pl.when(m + 2 < blocks)
         def _():
             for copy in m_copies(m + 2):
                 copy.start()
+
+    def gather(place):
+        j = groups - 1 - place
+
+        @pl.when(j > 0)
+        def _():
+            o_copy(j).wait()
+            g_copy(j).wait_send()
+
+        expert = flip(me, j, groups)
+        rows_back = jnp.dot(masks[j], returned[j], preferred_element_type=jnp.float32)
+        comb[...] += column(shares, expert) * rows_back
 
     def start_unit(u):
         big, place, j, b = split(u)
@@ -274,9 +276,13 @@
 
             out_copy(slot).start()
 
-        gate = came[1, slot, :, 0:COLS].astype(jnp.float32)
-        up = came[1, slot, :, COLS : 2 * COLS].astype(jnp.float32)
-        back = came[1, slot, :, 2 * COLS :].astype(jnp.float32)
+        real = lax.broadcasted_iota(jnp.int32, (rows, COLS), 0) < cap
+
+        def part(q):
+            cut = slice(q * COLS, (q + 1) * COLS)
+            return jnp.where(real, came[1, slot, :, cut].astype(jnp.float32), 0.0)
+
+        gate, up, back = part(0), part(1), part(2)
         sig = jax.nn.sigmoid(gate)
         hidden = (gate * sig * up).astype(jnp.bfloat16)
         gate_grad = (back * up * sig * (1.0 + gate * (1.0 - sig))).astype(jnp.bfloat16)
@@ -321,6 +327,10 @@
         def _():
             adam(m, b)
 
+        @pl.when((big == passes - 1) & (b == SUB // 2) & (place >= 2))
+        def _():
+            gather(place - 2)
+
     def step(i, _):
         @pl.when(i < groups)
         def _():
@@ -342,27 +352,16 @@
 
     lax.fori_loop(0, units + LAG * (line - 1), step, 0)
 
-    comb[...] = jnp.zeros_like(comb)
-
-    def gather(place, _):
-        j = groups - 1 - place
-
-        @pl.when(j > 0)
-        def _():
-            o_copy(j).wait()
-            g_copy(j).wait_send()
-
-        expert = flip(me, j, groups)
-        rows_back = jnp.dot(masks[j], returned[j], preferred_element_type=jnp.float32)
-        comb[...] += column(shares, expert) * rows_back
-        return 0
-
-    lax.fori_loop(0, groups, gather, 0)
+    for place in range(groups - min(groups, 2), groups):
+        gather(jnp.int32(place))
     combined[...] = comb[...].astype(jnp.bfloat16)
 
-    settle(blocks - 1)
     for m in (blocks - 2, blocks - 1):
-        u_store(m).wait()
+        keep, give = u_copies(jnp.int32(m))
+        keep.wait()
+        give.wait_send()
+    for m in range(blocks):
+        u_copies(jnp.int32(m))[1].wait_recv()
     for back in range(min(ring, units)):
         in_copy((units - 1 - back) % ring).wait_send()
 
@@ -370,6 +369,32 @@
     def _():
         for u in (units - 2, units - 1):
             out_copy(u % ring).wait_send()
+
+
+def pick(parts, flags, combined, both_steps, out, update, held, c_sem, in_sem, out_sem):
+    rung = lax.div(lax.axis_index("expert"), 2)
+    side = lax.rem(flags[rung], 2)
+    span = update.shape[2] // parts
+    to_out = pltpu.make_async_copy(combined, out, c_sem)
+    to_out.start()
+
+    def cut(p):
+        return pl.ds(p * span, span)
+
+    def fetch(p):
+        return pltpu.make_async_copy(both_steps.at[side, :, cut(p), :], held.at[p], in_sem.at[p])
+
+    def store(p):
+        return pltpu.make_async_copy(held.at[p], update.at[0, :, cut(p), :], out_sem.at[p])
+
+    for p in range(parts):
+        fetch(p).start()
+    for p in range(parts):
+        fetch(p).wait()
+        store(p).start()
+    for p in range(parts):
+        store(p).wait()
+    to_out.wait()
 
 
 def body(tokens, grad_out, routes, route_weights, swap_flags, weights, first_moment, second_moment):
@@ -380,23 +405,19 @@
     rows = -(-cap // 16) * 16
     passes = hidden_width // (COLS * SUB)
     blocks = passes * SUB
-    ring = LAG * (line - 1) + 3
-    me = lax.axis_index("expert")
-    paired = jnp.repeat(jnp.bitwise_and(swap_flags, 1), 2)
-    traded = jnp.sum(jnp.where(jnp.arange(groups) == me, paired, 0))
-    trade = jnp.broadcast_to(traded.astype(jnp.int32), (16, width))
+    ring = max(LAG * (line - 1) + 3, 2 * LAG + 5)
     bf, f32 = jnp.bfloat16, jnp.float32
     dma = pltpu.SemaphoreType.DMA
     whole = pl.BlockSpec(memory_space=pltpu.VMEM)
     left = pl.BlockSpec(memory_space=pl.ANY)
     flops = 2 * groups * rows * width * hidden_width * 7
-    combined, update = pl.pallas_call(
-        functools.partial(kernel, groups, line, ring, passes),
+    combined, both_steps = pl.pallas_call(
+        functools.partial(kernel, groups, line, ring, passes, cap),
         out_shape=(
             jax.ShapeDtypeStruct((toks, width), bf),
-            jax.ShapeDtypeStruct(weights.shape, bf),
+            jax.ShapeDtypeStruct((2,) + weights.shape[1:], bf),
         ),
-        in_specs=[whole] * 5 + [left] * 3,
+        in_specs=[whole] * 4 + [left] * 3,
         out_specs=(whole, left),
         scratch_shapes=[
             pltpu.VMEM((toks, 128), f32),
@@ -416,12 +437,11 @@
             pltpu.VMEM((2, 3, COLS, width), bf),
             pltpu.VMEM((2, 3, COLS, width), bf),
             pltpu.VMEM((2, 3, COLS, width), bf),
-            pltpu.VMEM((2, 3, COLS, width), bf),
             pltpu.VMEM((toks, width), f32),
             dma((groups,)), dma((groups,)), dma((groups,)), dma((groups,)),
             dma((groups,)), dma((groups,)),
             dma((ring,)), dma((2, ring)), dma((ring,)),
-            dma((blocks,)), dma((2, 2)), dma((2,)), dma((2,)), dma((2,)),
+            dma((blocks,)), dma((2, 2)), dma((2,)), dma((blocks,)), dma((2,)),
         ],
         compiler_params=pltpu.CompilerParams(
             has_side_effects=True, vmem_limit_bytes=66_000_000
@@ -429,8 +449,22 @@
         cost_estimate=pl.CostEstimate(
             flops=flops, bytes_accessed=8 * weights.size, transcendentals=0
         ),
-    )(tokens, grad_out, routes, route_weights, trade, weights, first_moment, second_moment)
-    return combined, update
+    )(tokens, grad_out, routes.T, route_weights.T, weights, first_moment, second_moment)
+    parts = 6
+    return pl.pallas_call(
+        functools.partial(pick, parts),
+        out_shape=(
+            jax.ShapeDtypeStruct((toks, width), bf),
+            jax.ShapeDtypeStruct(weights.shape, bf),
+        ),
+        in_specs=[pl.BlockSpec(memory_space=pltpu.SMEM), whole, left],
+        out_specs=(left, left),
+        scratch_shapes=[
+            pltpu.VMEM((parts, 3, hidden_width // parts, width), bf),
+            dma, dma((parts,)), dma((parts,)),
+        ],
+        compiler_params=pltpu.CompilerParams(vmem_limit_bytes=66_000_000),
+    )(swap_flags, combined, both_steps)
 
 
 def solution(mesh):

time: 397 us -> 356 us (0.90)
  Pallas kernels: 380 us -> 355 us
  local copies, waits for them, and re-layouts: 14.8 us -> 0 us
    pallas_call x1 -> x2, Pallas kernels: 380 us -> 355 us  [the longest x1 347 us: body(): pl.pallas_call(functools.partial(kernel, groups, line, ring, passes, cap)...]
    unnamed x4 -> x0, local copies, waits for them, and re-layouts: 13.5 us -> none
where the time goes in v1:
time: 356 us
  Pallas kernels  355 us (100%)
    pallas_call x1, Pallas kernels, body(): pl.pallas_call(functools.partial(kernel, groups, line, ring, passes, cap)...  347 us
    pallas_call x1, Pallas kernels, body(): pl.pallas_call(functools.partial(pick, parts), out_shape=(jax.ShapeDtypeS...  8.61 us

profile of v1, /device:TPU:0, one launch (start us, length us, event | category | flops | bytes accessed | tf_op | source)
XLA Modules:
  0.0 355.9 jit_solution(675205824210665150)
XLA Ops:
  0.6 346.7 %shard_map.95 = (bf16[320,1024]{1,0:T(8,128)(2,1)}, bf16[2,3,1536,1024]{3,2,1,0:T(8,128)(2,1)}) custom-call(bf16[320,1024]{1,0:T(8,128)(2,1)} %tokens.1, bf16[320,1024]{1,0:T(8,128)(2,1)} %grads.1, s32[4,320]{1,0:T(4,128)} %bitcast.2, f32[4,320]{1,0:T(4,128)} %bitcast.3, bf16[1,3,1536,1024]{3,2,1,0:T(8,128)(2,1)} %weights.1, ...), custom_call_target="tpu_custom_call" | custom-call | flops 36641439744 | bytes 37748736 | tf_op jit(solution)/shard_map/pallas_call | solution.py:414
  347.3 8.6 %shard_map.96 = (bf16[320,1024]{1,0:T(8,128)(2,1)}, bf16[1,3,1536,1024]{3,2,1,0:T(8,128)(2,1)}) custom-call(s32[4]{0:T(128)} %flags.1, bf16[320,1024]{1,0:T(8,128)(2,1)} %get-tuple-element.4.combined, bf16[2,3,1536,1024]{3,2,1,0:T(8,128)(2,1)} %get-tuple-element.5.both_steps), custom_call_target="tpu_custom_call" | custom-call | tf_op jit(solution)/shard_map/pallas_call | solution.py:454
